TPU v7x, 32 devices: a whole 2x2x4 slice. The times are simulated.
32 devices in a mesh: bal: 8 (over z, x), seq: 4 (over y, core).
Axes of the slice: x: 2, y: 2, z: 4, core: 2. Of those that a mesh axis runs over, the one named last changes fastest.
Arguments:
- tokens: bfloat16 [128, 64, 5120], P('bal', 'seq'), may hold values from -6 to 6
- w_qkv: bfloat16 [5120, 24, 384], P('bal', 'seq')
- q_gain: float32 [24, 128], P('seq')
- k_gain: float32 [24, 128], P('seq')
- modulation: float32 [8, 4, 2, 5120], P('bal'), may hold values from -3 to 3
- tile_owner: int32 [128], P('bal'), may hold values from 0 to 7, as said below
- clip_dims: int32 [8, 4, 3], P('bal'), may hold values from 0 to 4, as said below
Outputs:
- attn_out: bfloat16 [128, 64, 3072], P('bal', 'seq')
Inputs may be any that keep to these rules, and one draw needn't show every extreme that they name: `tile_owner`: each owner is named by exactly 16 tiles. The 16 tiles of one bal index name any owner at most 2 times, and in every draw some owner exactly 2 times. `clip_dims`: for each owner the clips' products f h w add up to 16; entries after its last clip are 0; a clip spans at most 2 tile frames, 3 tile rows and 4 tile columns and has 4 tiles or more.
All inputs are finite; a program needn't handle non-finite values.
Results may differ from a plain program's by a relative error of at most 0.006.
Values may be sent and summed in bfloat16 or wider, within the bound.
No kernel may reach another device: no remote copies, remote signals or barrier semaphores. Data moves between devices by JAX's collectives and lax.ppermute only.
A program may use at most 128 MiB of HBM per device.

v0:
```python
import jax
import jax.numpy as jnp
from jax import lax
from jax.sharding import PartitionSpec as P

HEADS = 24
TILES_OWN = 16
eps_norm = 1e-06
score_fill = -1e30


def tile_layout(clip_shape):
    frames_of = clip_shape[:, 0]
    rows_of = clip_shape[:, 1]
    cols_of = clip_shape[:, 2]
    clip_sizes = frames_of * rows_of * cols_of
    clip_ends = jnp.cumsum(clip_sizes)
    clip_starts = clip_ends - clip_sizes
    local_index = jnp.arange(TILES_OWN, dtype=jnp.int32)
    member = jnp.sum((local_index[:, None] >= clip_ends[None, :]).astype(jnp.int32), axis=1)
    onehot = member[:, None] == jnp.arange(clip_shape.shape[0], dtype=jnp.int32)[None, :]

    def select_clip(values):
        return jnp.sum(jnp.where(onehot, values[None, :], 0), axis=1)

    offset = local_index - select_clip(clip_starts)
    height = jnp.maximum(select_clip(rows_of), 1)
    width_tiles = jnp.maximum(select_clip(cols_of), 1)
    frame_index = offset // (height * width_tiles)
    row_index = offset // width_tiles % height
    column = offset % width_tiles

    def within_one(coords):
        return jnp.abs(coords[:, None] - coords[None, :]) <= 1

    tile_mask = (
        (member[:, None] == member[None, :])
        & within_one(frame_index)
        & within_one(row_index)
        & within_one(column)
    )
    return (onehot, tile_mask)


def clip_rows(onehot, mod_table):
    picked = jnp.sum(jnp.where(onehot[:, :, None, None], mod_table[None], 0.0), axis=1)
    return (picked[:, 0], picked[:, 1])


def modulate(pieces, shift_rows, scale_rows):
    values = pieces.astype(jnp.float32)
    center = jnp.mean(values, axis=-1, keepdims=True)
    spread = jnp.mean(jnp.square(values - center), axis=-1, keepdims=True)
    normal = (values - center) * lax.rsqrt(spread + eps_norm)
    return (normal * (1.0 + scale_rows[:, None, :]) + shift_rows[:, None, :]).astype(jnp.bfloat16)


def attend(q_block, key_rows, values, block_mask):
    scores = jnp.einsum(
        "qhd,khd->hqk", q_block, key_rows, preferred_element_type=jnp.float32
    ) * key_rows.shape[2] ** (-0.5)
    scores = jnp.where(block_mask[None], scores, score_fill)
    largest = jnp.max(scores, axis=-1, keepdims=True)
    exp_scores = jnp.exp(scores - largest)
    totals = jnp.sum(exp_scores, axis=-1, keepdims=True)
    weights = (exp_scores / totals).astype(jnp.bfloat16)
    return jnp.einsum("hqk,khd->qhd", weights, values, preferred_element_type=jnp.float32)


def per_device(tokens, w_qkv, q_gain, k_gain, modulation, tile_owner, clip_dims):
    groups = lax.axis_size("bal")
    owned_tiles, piece_len, width_model = tokens.shape
    capacity = owned_tiles // min(groups, owned_tiles)
    slot_count = groups * capacity
    flat_weight = w_qkv.reshape(w_qkv.shape[0], -1)
    slot_ids = jnp.arange(slot_count, dtype=jnp.int32)
    earlier = jnp.arange(owned_tiles)[:, None] > jnp.arange(owned_tiles)[None, :]
    slot_rank = jnp.sum((tile_owner[:, None] == tile_owner[None, :]) & earlier, axis=1)
    target = tile_owner * capacity + slot_rank
    route_onehot = (slot_ids[:, None] == target[None, :]).astype(jnp.bfloat16)
    outbound = jnp.dot(
        route_onehot, tokens.reshape(owned_tiles, -1), preferred_element_type=jnp.float32
    ).astype(jnp.bfloat16)
    outbound = outbound.reshape(groups, capacity, piece_len, width_model)
    filled = jnp.sum(route_onehot, axis=1).reshape(groups, capacity)
    arrived, arrived_flags = (
        lax.all_to_all(outbound, "bal", split_axis=0, concat_axis=0, tiled=True),
        lax.all_to_all(filled, "bal", split_axis=0, concat_axis=0, tiled=True),
    )
    live_slots = arrived_flags.reshape(slot_count) > 0.5
    position = jnp.cumsum(live_slots.astype(jnp.int32)) - 1
    collect = ((jnp.arange(TILES_OWN)[:, None] == position[None, :]) & live_slots[None, :]).astype(
        jnp.bfloat16
    )
    compact = jnp.dot(
        collect, arrived.reshape(slot_count, -1), preferred_element_type=jnp.float32
    ).astype(jnp.bfloat16)
    compact = compact.reshape(TILES_OWN, piece_len, width_model)
    onehot, tile_mask = tile_layout(clip_dims[0])
    shift_rows, scale_rows = clip_rows(onehot, modulation[0])
    whole_tiles = lax.all_gather(compact, "seq", axis=1, tiled=True)
    normed = modulate(whole_tiles, shift_rows, scale_rows)
    tile_len = normed.shape[1]
    token_rows = normed.reshape(-1, width_model)
    total_tokens = token_rows.shape[0]
    per_dev_heads = q_gain.shape[0]
    projected = jnp.dot(
        token_rows,
        lax.all_gather(flat_weight, "bal", axis=0, tiled=True),
        preferred_element_type=jnp.float32,
    )
    projected = projected.reshape(total_tokens, per_dev_heads, 3, -1)
    query = projected[:, :, 0]
    keyed = projected[:, :, 1]
    valued = projected[:, :, 2].astype(jnp.bfloat16)
    sums_q, sums_k = lax.psum(
        (jnp.sum(jnp.square(query), axis=(1, 2)), jnp.sum(jnp.square(keyed), axis=(1, 2))), "seq"
    )
    features = HEADS * query.shape[2]
    q_normed = (
        query * lax.rsqrt(sums_q / features + eps_norm)[:, None, None] * q_gain[None]
    ).astype(jnp.bfloat16)
    k_normed = (
        keyed * lax.rsqrt(sums_k / features + eps_norm)[:, None, None] * k_gain[None]
    ).astype(jnp.bfloat16)
    token_mask = jnp.repeat(jnp.repeat(tile_mask, tile_len, axis=0), tile_len, axis=1)
    block_rows = min(512, total_tokens)
    outputs = []
    for block_start in range(0, total_tokens, block_rows):
        outputs.append(
            attend(
                q_normed[block_start : block_start + block_rows],
                k_normed,
                valued,
                token_mask[block_start : block_start + block_rows],
            )
        )
    attended = jnp.concatenate(outputs, axis=0).astype(jnp.bfloat16)
    head_major = attended.reshape(TILES_OWN, tile_len, -1)
    spread_back = jnp.dot(
        collect.T, head_major.reshape(TILES_OWN, -1), preferred_element_type=jnp.float32
    ).astype(jnp.bfloat16)
    spread_back = spread_back.reshape(groups, capacity, tile_len, -1)
    returned = lax.all_to_all(
        lax.all_to_all(spread_back, "bal", split_axis=0, concat_axis=0, tiled=True),
        "seq",
        split_axis=2,
        concat_axis=3,
        tiled=True,
    )
    result = jnp.dot(
        route_onehot.T, returned.reshape(slot_count, -1), preferred_element_type=jnp.float32
    ).astype(jnp.bfloat16)
    return result.reshape(owned_tiles, piece_len, -1)


def solution(mesh):
    return jax.shard_map(
        per_device,
        mesh=mesh,
        in_specs=(
            P("bal", "seq", None),
            P("bal", "seq", None),
            P("seq", None),
            P("seq", None),
            P("bal", None, None, None),
            P("bal"),
            P("bal", None, None),
        ),
        out_specs=P("bal", "seq", None),
        check_vma=False,
    )
```

profile of v0, /device:TPU:0, one launch (start us, length us, event | category | flops | bytes accessed | tf_op | source)
XLA Modules:
  0.0 808.7 jit_solution(5014179867423074362)
XLA Ops:
  6.5 0.9 convert_reduce_fusion.1
  7.4 0.7 multiply_add_fusion
  8.2 0.7 all_to_all.30
  8.9 7.3 all-to-all-start
  16.2 3.2 copy.84
  19.4 0.8 convolution_convert_fusion.1
  20.2 2.9 copy.85
  23.1 6.0 all-to-all-start.1
  29.6 58.5 %all-to-all-done.1 = bf16[8,2,16,5120]{3,2,1,0:T(8,128)(2,1)S(1)} async-done(((bf16[8,2,16,5120]{3,2,1,0:T(8,128)(2,1)}), bf16[8,2,16,5120]{3,2,1,0:T(8,128)(2,1)S(1)}, u32[]{:S(2)}, u32[]{:S(2)}) %all-to-all-start.1) | async-done | bytes 2621472 | tf_op jit(solution)/shard_map/all_to_all | solution.py:87
  88.1 1.4 copy.86
  89.5 0.8 convolution_convert_fusion
  90.3 2.9 copy.87
  93.3 0.6 all-gather.5.cloned.1.call-start
  93.9 3.5 copy.67
  98.8 0.9 copy.68
  100.1 0.9 copy.71
  101.1 0.3 select_reduce_fusion
  101.4 61.3 %all-gather.3.cloned.1.call-done = bf16[16,64,5120]{2,1,0:T(8,128)(2,1)} async-done(((bf16[16,16,5120]{2,1,0:T(8,128)(2,1)}), bf16[16,64,5120]{2,1,0:T(8,128)(2,1)}) %all-gather.3.cloned.1.call-update) | async-done | bytes 10485776 | tf_op jit(solution)/shard_map/all_gather | solution.py:101
  162.7 5.6 convert_reduce_fusion
  168.3 1.3 copy-done
  169.6 2.8 fusion.4
  172.5 8.3 %fusion.7 = bf16[16,64,5120]{2,1,0:T(8,128)(2,1)} fusion(bf16[16,64,5120]{2,1,0:T(8,128)(2,1)S(1)} %copy-done, f32[16,5120]{1,0:T(8,128)S(1)} %get-tuple-element.16, f32[16,5120]{1,0:T(8,128)S(1)} %get-tuple-element.15, f32[16,64]{1,0:T(8,128)S(1)} %add_rsqrt_fusion, f32[16,64]{1,0:T(8,128)S(1)} %broadcast_multiply_fusion), kind=kLoop, calls=%fused_computation.13 | loop fusion | flops 31457280 | bytes 21635072 | tf_op jit(solution)/shard_map/convert_element_type | solution.py:55
  180.8 434.4 %all-gather.5.cloned.1.call-done = bf16[5120,2304]{0,1:T(8,128)(2,1)} async-done(((bf16[640,2304]{0,1:T(8,128)(2,1)}), bf16[5120,2304]{0,1:T(8,128)(2,1)}) %all-gather.5.cloned.1.call-update) | async-done | bytes 23592976 | tf_op jit(solution)/shard_map/all_gather | solution.py:109
  615.1 29.6 %fusion.53 = f32[1024,6,3,128]{0,3,2,1:T(8,128)S(1)} fusion(bf16[1024,5120,1,1]{1,0,3,2:T(8,128)(2,1)} %bitcast.70, bf16[6,3,128,5120]{3,2,1,0:T(8,128)(2,1)} %bitcast.86), kind=kOutput, calls=%fused_computation.106 | convolution fusion | flops 24159191040 | bytes 43515904 | tf_op jit(solution)/shard_map/dot_general | solution.py:107
  644.8 3.6 copy-done.1
  648.4 0.6 multiply_reduce_fusion
  649.1 6.5 all-reduce
  655.6 2.4 multiply_convert_fusion.1
  658.0 8.4 %fusion.25 = f32[6,512,1024]{2,1,0:T(8,128)} fusion(bf16[1024,6,128]{0,2,1:T(8,128)(2,1)S(1)} %multiply_convert_fusion.1, f32[1024,6,3,128]{0,3,2,1:T(8,128)} %copy-done.1, f32[6,128]{1,0:T(8,128)S(1)} %copy-done.4, f32[1024]{0:T(1024)S(1)} %get-tuple-element.27), kind=kOutput, calls=%fused_computation.46 | convolution fusion | flops 807665664 | bytes 16523264 | tf_op jit(solution)/shard_map/qhd,khd->hqk/dot_general | solution.py:59
  666.5 6.5 fusion.23
  672.9 17.2 %fusion.52 = (f32[6,512]{1,0:T(8,128)S(1)}, f32[6,512,1024]{2,1,0:T(8,128)}) fusion(f32[6,512,1024]{2,1,0:T(8,128)} %fusion.25, pred[512,1024]{1,0:T(8,128)(4,1)S(1)} %copy.68), kind=kOutput, calls=%fused_computation.105 | output fusion | flops 18875392 | bytes 25702400 | tf_op jit(solution)/shard_map/sub | solution.py:64
  690.1 6.9 fusion.21
  697.0 16.5 %fusion.51 = (f32[6,512]{1,0:T(8,128)S(1)}, f32[6,512,1024]{2,1,0:T(8,128)}) fusion(f32[6,512,1024]{2,1,0:T(8,128)} %fusion.23, pred[512,1024]{1,0:T(8,128)(4,1)S(1)} %copy.71), kind=kOutput, calls=%fused_computation.104 | output fusion | flops 18875392 | bytes 25702400 | tf_op jit(solution)/shard_map/sub | solution.py:64
  713.6 6.9 fusion.22
  720.5 1.3 pad_maximum_fusion
  721.8 3.2 copy.74
  725.1 2.8 convert_element_type.80
  727.9 2.0 convolution_convert_fusion.3
  730.0 0.3 copy.88
  730.3 1.6 copy.75
  731.9 40.6 %all_to_all.35 = bf16[8,2,64,768]{3,1,2,0:T(2,128)(2,1)S(1)} all-to-all(bf16[8,2,64,768]{3,1,2,0:T(2,128)(2,1)S(1)} %copy.75), channel_id=1, replica_groups=mesh['bal'=8,'seq'=4] {'bal'}, dimensions={0} | all-to-all | bytes 3145728 | tf_op jit(solution)/shard_map/all_to_all | solution.py:145
  772.5 1.1 copy.76
  773.6 22.6 %all_to_all.36 = bf16[8,2,64,768]{3,1,0,2:T(2,128)(2,1)S(1)} all-to-all(bf16[8,2,64,768]{3,1,0,2:T(2,128)(2,1)S(1)} %copy.76), channel_id=1, replica_groups=mesh['bal'=8,'seq'=4] {'seq'}, dimensions={2} | all-to-all | bytes 3145728 | tf_op jit(solution)/shard_map/all_to_all | solution.py:144
  796.3 0.5 copy.77
  796.7 0.8 copy.78
  797.6 1.2 reshape.305
  798.7 0.6 convolution_convert_fusion.2
  799.4 2.0 copy.89
  (51 shorter events, 2.4 us)
Async XLA Ops:
  8.9 14.2 %all-to-all-start = ((bf16[8,1,2]{2,1,0:T(2,128)(2,1)}), bf16[8,1,2]{2,1,0:T(2,128)(2,1)S(1)}, u32[]{:S(2)}, u32[]{:S(2)}) async-start(bf16[8,1,2]{2,1,0:T(2,128)(2,1)} %all_to_all.30), calls=%async_computation | async-start | bytes 8192 | tf_op jit(solution)/shard_map/all_to_all | solution.py:88
  23.1 64.9 %all-to-all-start.1 = ((bf16[8,2,16,5120]{3,2,1,0:T(8,128)(2,1)}), bf16[8,2,16,5120]{3,2,1,0:T(8,128)(2,1)S(1)}, u32[]{:S(2)}, u32[]{:S(2)}) async-start(bf16[8,2,16,5120]{3,2,1,0:T(8,128)(2,1)} %bitcast.27), calls=%async_computation.1 | async-start | bytes 5242880 | tf_op jit(solution)/shard_map/all_to_all | solution.py:87
  29.1 133.5 %all-gather.3.cloned.1.call-start = ((), (), s32[]{:S(2)}) async-start(), calls=%async_computation.4 | async-start | bytes 13107200 | tf_op jit(solution)/shard_map/all_gather | solution.py:101
  90.3 3.5 copy-start.2
  93.3 4.1 copy-start.6
  93.3 521.8 %all-gather.5.cloned.1.call-start = ((), (), s32[]{:S(2)}) async-start(), calls=%async_computation.5 | async-start | bytes 26542080 | tf_op jit(solution)/shard_map/all_gather | solution.py:109
  97.4 3.7 copy-start.3
  162.7 7.0 copy-start
  644.8 3.6 copy-start.1
  648.4 7.2 copy-start.5
  649.0 8.9 %copy-start.4 = (f32[6,128]{1,0:T(8,128)S(1)}, f32[6,128]{1,0:T(8,128)}, u32[]{:S(2)}) copy-start(f32[6,128]{1,0:T(8,128)} %param.10) | copy-start | bytes 9220
  655.6 10.8 %slice-start = ((s8[9437184]{0:T(1024)(128)(4,1)}), s8[4194304]{0:T(1024)(128)(4,1)S(1)}, s32[]{:S(2)}) async-start(s8[9437184]{0:T(1024)(128)(4,1)} %bitcast.67), calls=%async_computation.6 | async-start | bytes 8388608
  658.0 8.4 %slice-start.1 = ((s8[9437184]{0:T(1024)(128)(4,1)}), s8[4194304]{0:T(1024)(128)(4,1)S(1)}, s32[]{:S(2)}) async-start(s8[9437184]{0:T(1024)(128)(4,1)} %bitcast.67), calls=%async_computation.7 | async-start | bytes 8388608
  658.0 8.4 %slice-start.2 = ((s8[9437184]{0:T(1024)(128)(4,1)}), s8[1048576]{0:T(1024)(128)(4,1)S(1)}, s32[]{:S(2)}) async-start(s8[9437184]{0:T(1024)(128)(4,1)} %bitcast.67), calls=%async_computation.8 | async-start | bytes 2097152
Sparse Core Ops, SparseCore 0:
  93.4 69.2 all-gather.2
  164.2 450.8 all-gather.4
where the time goes:
time: 815 us; the launch traced here: 809 us
  waiting for transfers between devices  554 us (68%)
  blocking collectives  69.8 us (9%)
  matrix products  62.7 us (8%)
  other arithmetic  57.9 us (7%)
  local copies, waits for them, and re-layouts  36.1 us (4%)
  between operations  14.2 us (2%)
  starting transfers between devices  13.9 us (2%)
    all_gather x1, waiting for transfers between devices, per_device(): lax.all_gather(flat_weight, 'bal', axis=0, tiled=True)  434 us
    all_gather x1, waiting for transfers between devices, per_device(): whole_tiles = lax.all_gather(compact, 'seq', axis=1, tiled=True)  61.3 us
    all_to_all x1, waiting for transfers between devices, per_device(): lax.all_to_all(outbound, 'bal', split_axis=0, concat_axis=0, tiled=True)  58.5 us
    all_to_all x1, blocking collectives, per_device(): lax.all_to_all(spread_back, 'bal', split_axis=0, concat_axis=0, tiled=True)  40.6 us
    sub x2, other arithmetic, attend(): exp_scores = jnp.exp(scores - largest)  33.7 us
    dot_general x1, matrix products, per_device(): jnp.dot(token_rows, lax.all_gather(flat_weight, 'bal', axis=0, tiled=True...  29.6 us
    all_to_all x1, blocking collectives, per_device(): lax.all_to_all(lax.all_to_all(spread_back, 'bal', split_axis=0, concat_ax...  22.6 us
    unnamed x28, local copies, waits for them, and re-layouts  21.4 us
  transfers between devices with their start and end apart: 4, of which 3 were waited for; matrix products, arithmetic and copies ran while one was open for 4% of the time, Pallas kernels for 0%

commit v1 on v0

--- a/solution.py
+++ b/solution.py
@@ -1,3 +1,4 @@
+import functools
 import jax
 import jax.numpy as jnp
 from jax import lax
@@ -7,6 +8,39 @@
 TILES_OWN = 16
 eps_norm = 1e-06
 score_fill = -1e30
+
+
+def obtain_screen(local_values, axis_k):
+    local_values = jnp.moveaxis(local_values, 0, axis_k)
+    mat_out = local_values.shape
+    return local_values.reshape(
+        *mat_out[:axis_k], mat_out[axis_k] * mat_out[axis_k + 1], *mat_out[axis_k + 2 :]
+    )
+
+
+def _lay_flows(sample, mesh_dim, d_out):
+    axis_total = lax.axis_size(mesh_dim)
+    vals = tuple(((no, (no + 1) % axis_total) for no in range(axis_total)))
+    found = tuple(((s, w) for w, s in vals))
+    val2, part_now = ([], [])
+    d = 0
+    while d < axis_total - 1:
+        if d % 2 == 0:
+            mid_arr = lax.ppermute(val2[-1] if val2 else sample, mesh_dim, vals)
+            val2.append(mid_arr)
+        else:
+            shaped = lax.ppermute(part_now[-1] if part_now else sample, mesh_dim, found)
+            part_now.append(shaped)
+        d = d + 1
+    h_now = jnp.stack([*val2[::-1], sample, *part_now], axis=0)
+    placed = lax.axis_index(mesh_dim)
+    e_now = len(val2)
+    w1 = placed - e_now
+    h_now = h_now[(jnp.arange(axis_total) - w1) % axis_total]
+    return obtain_screen(h_now, d_out)
+
+
+supply_all_the_edges = functools.partial(_lay_flows, mesh_dim="bal", d_out=0)
 
 
 def tile_layout(clip_shape):
@@ -105,9 +139,7 @@
     total_tokens = token_rows.shape[0]
     per_dev_heads = q_gain.shape[0]
     projected = jnp.dot(
-        token_rows,
-        lax.all_gather(flat_weight, "bal", axis=0, tiled=True),
-        preferred_element_type=jnp.float32,
+        token_rows, supply_all_the_edges(flat_weight), preferred_element_type=jnp.float32
     )
     projected = projected.reshape(total_tokens, per_dev_heads, 3, -1)
     query = projected[:, :, 0]

time: 815 us -> 815 us (level)
  waiting for transfers between devices: 554 us -> 433 us
  local copies, waits for them, and re-layouts: 36.1 us -> 119 us
  other arithmetic: 57.9 us -> 76.2 us
  starting transfers between devices: 13.9 us -> 28.6 us
    all_gather x1 -> x0, waiting for transfers between devices: 434 us -> none  [per_device(): lax.all_gather(flat_weight, 'bal', axis=0, tiled=True)]
    ppermute x0 -> x7, waiting for transfers between devices: none -> 378 us  [the longest x4 378 us: _lay_flows(): mid_arr = lax.ppermute(val2[-1] if val2 else sample, mesh_dim, vals)]
    all_gather x1, waiting for transfers between devices: 61.3 us -> 0.01 us  [per_device(): whole_tiles = lax.all_gather(compact, 'seq', axis=1, tiled=True)]
    all_to_all x1, waiting for transfers between devices: 58.5 us -> 0.01 us  [per_device(): lax.all_to_all(outbound, 'bal', split_axis=0, concat_axis=0, tiled=True)]
    all_to_all x1, waiting for transfers between devices: 0.01 us -> 54.5 us  [per_device(): lax.all_to_all(filled, 'bal', split_axis=0, concat_axis=0, tiled=True)]
    reshape x0 -> x2, local copies, waits for them, and re-layouts: none -> 33.2 us  [the longest x1 29.6 us: obtain_screen(): local_values.reshape(*mat_out[:axis_k], mat_out[axis_k] * mat_out[axis_k...]
    gather x0 -> x3, local copies, waits for them, and re-layouts: none -> 30 us  [_lay_flows(): h_now = h_now[(jnp.arange(axis_total) - w1) % axis_total]]
    unnamed x1 -> x2, other arithmetic: 0.01 us -> 19.5 us
  transfers between devices with their start and end apart: 4 -> 10, of which waited for: 3 -> 4; matrix products, arithmetic and copies ran while one was open for 4% -> 14% of each run, Pallas kernels for 0% -> 0%
where the time goes in v1:
time: 815 us; the launch traced here: 807 us
  waiting for transfers between devices  433 us (53%)
  local copies, waits for them, and re-layouts  119 us (15%)
  other arithmetic  76.2 us (9%)
  blocking collectives  73.6 us (9%)
  matrix products  62.8 us (8%)
  starting transfers between devices  28.6 us (4%)
  between operations  14.1 us (2%)
    ppermute x4, waiting for transfers between devices, _lay_flows(): mid_arr = lax.ppermute(val2[-1] if val2 else sample, mesh_dim, vals)  378 us
    all_to_all x1, waiting for transfers between devices, per_device(): lax.all_to_all(filled, 'bal', split_axis=0, concat_axis=0, tiled=True)  54.5 us
    all_to_all x1, blocking collectives, per_device(): lax.all_to_all(spread_back, 'bal', split_axis=0, concat_axis=0, tiled=True)  45.3 us
    unnamed x51, local copies, waits for them, and re-layouts  36.3 us
    sub x2, other arithmetic, attend(): exp_scores = jnp.exp(scores - largest)  33.9 us
    gather x3, local copies, waits for them, and re-layouts, _lay_flows(): h_now = h_now[(jnp.arange(axis_total) - w1) % axis_total]  30 us
    dot_general x1, matrix products, per_device(): jnp.dot(token_rows, supply_all_the_edges(flat_weight), preferred_element_...  29.7 us
    reshape x1, local copies, waits for them, and re-layouts, obtain_screen(): local_values.reshape(*mat_out[:axis_k], mat_out[axis_k] * mat_out[axis_k...  29.6 us
  transfers between devices with their start and end apart: 10, of which 4 were waited for; matrix products, arithmetic and copies ran while one was open for 14% of the time, Pallas kernels for 0%

profile of v1, /device:TPU:0, one launch (start us, length us, event | category | flops | bytes accessed | tf_op | source)
XLA Modules:
  0.0 806.6 jit_solution(10772905506142008500)
XLA Ops:
  6.5 4.1 copy.87
  10.7 3.6 copy.88
  14.3 3.0 collective-permute-start
  18.2 4.9 all-to-all-start
  23.1 3.2 copy.109
  27.1 2.9 copy.110
  30.0 54.5 %all-to-all-done = bf16[8,1,2]{2,1,0:T(2,128)(2,1)S(1)} async-done(((bf16[8,1,2]{2,1,0:T(2,128)(2,1)}), bf16[8,1,2]{2,1,0:T(2,128)(2,1)S(1)}, u32[]{:S(2)}, u32[]{:S(2)}) %all-to-all-start) | async-done | bytes 64 | tf_op jit(solution)/shard_map/all_to_all | solution.py:122
  84.5 4.4 all-to-all-start.1
  90.9 2.9 collective-permute-start.4
  93.8 149.6 %collective-permute-done.1 = bf16[640,2304]{1,0:T(8,128)(2,1)} collective-permute-done((bf16[640,2304]{1,0:T(8,128)(2,1)}, bf16[640,2304]{1,0:T(8,128)(2,1)}, u32[]{:S(2)}, u32[]{:S(2)}) %collective-permute-start.1) | collective-permute-done | bytes 2949152 | tf_op jit(solution)/shard_map/ppermute | solution.py:29
  243.4 2.5 collective-permute-start.2
  246.3 3.2 copy.111
  250.3 3.0 copy.112
  253.4 2.6 collective-permute-start.5
  256.0 115.6 %collective-permute-done.2 = bf16[640,2304]{1,0:T(8,128)(2,1)} collective-permute-done((bf16[640,2304]{1,0:T(8,128)(2,1)}, bf16[640,2304]{1,0:T(8,128)(2,1)}, u32[]{:S(2)}, u32[]{:S(2)}) %collective-permute-start.2) | collective-permute-done | bytes 2949152 | tf_op jit(solution)/shard_map/ppermute | solution.py:29
  371.6 2.6 collective-permute-start.3
  374.7 3.5 copy.91
  382.3 3.8 collective-permute-start.6
  386.1 113.1 %collective-permute-done.3 = bf16[640,2304]{1,0:T(8,128)(2,1)} collective-permute-done((bf16[640,2304]{1,0:T(8,128)(2,1)}, bf16[640,2304]{1,0:T(8,128)(2,1)}, u32[]{:S(2)}, u32[]{:S(2)}) %collective-permute-start.3) | collective-permute-done | bytes 2949152 | tf_op jit(solution)/shard_map/ppermute | solution.py:29
  499.2 2.0 bitcast_dynamic-update-slice_fusion.6
  501.2 2.2 bitcast_dynamic-update-slice_fusion.5
  503.4 2.0 bitcast_dynamic-update-slice_fusion.4
  505.4 2.0 bitcast_dynamic-update-slice_fusion.3
  507.7 2.0 bitcast_dynamic-update-slice_fusion.2
  509.7 2.0 bitcast_dynamic-update-slice_fusion.1
  511.9 8.8 %fusion.52 = (bf16[8,640,1152]{2,1,0:T(8,128)(2,1)}, bf16[8,640,1152]{2,1,0:T(8,128)(2,1)}) fusion(bf16[8,640,2304]{2,1,0:T(8,128)(2,1)S(1)} %bitcast_dynamic-update-slice_fusion), kind=kLoop, calls=%fused_computation.121 | loop fusion | bytes 47185920 | tf_op jit(solution)/shard_map/gather | solution.py:39
  520.8 10.7 %gather_fusion = bf16[8,640,1152]{2,1,0:T(8,128)(2,1)} fusion(bf16[8,640,1152]{2,1,0:T(8,128)(2,1)} %get-tuple-element.15, s32[1024]{0:T(1024)S(1)} %pad_clamp_fusion), kind=kCustom, calls=%fused_computation | custom fusion | bytes 23592992 | tf_op jit(solution)/shard_map/gather | solution.py:39
  531.5 10.5 %gather_fusion.1 = bf16[8,640,1152]{2,1,0:T(8,128)(2,1)} fusion(bf16[8,640,1152]{2,1,0:T(8,128)(2,1)} %get-tuple-element.16, s32[1024]{0:T(1024)S(1)} %pad_clamp_fusion), kind=kCustom, calls=%fused_computation.1 | custom fusion | bytes 23592992 | tf_op jit(solution)/shard_map/gather | solution.py:39
  542.0 19.5 %pad_maximum_fusion = bf16[8,640,2304]{2,1,0:T(8,128)(2,1)} fusion(bf16[8,640,1152]{2,1,0:T(8,128)(2,1)} %gather_fusion.1, bf16[8,640,1152]{2,1,0:T(8,128)(2,1)} %gather_fusion), kind=kLoop, calls=%fused_computation.12 | loop fusion | flops 47185920 | bytes 47185920
  561.4 29.6 %copy.92 = bf16[5120,2304]{0,1:T(8,128)(2,1)} copy(bf16[5120,2304]{1,0:T(8,128)(2,1)} %bitcast.85) | data formatting | bytes 47185920 | tf_op jit(solution)/shard_map/reshape | solution.py:16
  591.1 5.6 convert_reduce_fusion
  598.0 2.8 fusion.4
  600.9 8.2 %fusion.7 = bf16[16,64,5120]{2,1,0:T(8,128)(2,1)} fusion(bf16[16,64,5120]{2,1,0:T(8,128)(2,1)S(1)} %copy-done, f32[16,5120]{1,0:T(8,128)S(1)} %get-tuple-element.18, f32[16,5120]{1,0:T(8,128)S(1)} %get-tuple-element.17, f32[16,64]{1,0:T(8,128)S(1)} %add_rsqrt_fusion, f32[16,64]{1,0:T(8,128)S(1)} %broadcast_multiply_fusion), kind=kLoop, calls=%fused_computation.16 | loop fusion | flops 31457280 | bytes 21635072 | tf_op jit(solution)/shard_map/convert_element_type | solution.py:89
  609.1 29.7 %fusion.56 = f32[1024,6,3,128]{0,3,2,1:T(8,128)S(1)} fusion(bf16[1024,5120,1,1]{1,0,3,2:T(8,128)(2,1)} %bitcast.91, bf16[6,3,128,5120]{3,2,1,0:T(8,128)(2,1)} %bitcast.90), kind=kOutput, calls=%fused_computation.125 | convolution fusion | flops 24159191040 | bytes 43515904 | tf_op jit(solution)/shard_map/dot_general | solution.py:141
  638.8 3.6 copy-done.1
  643.1 5.8 all-reduce
  648.9 2.4 multiply_convert_fusion.1
  651.3 8.4 %fusion.25 = f32[6,512,1024]{2,1,0:T(8,128)} fusion(bf16[1024,6,128]{0,2,1:T(8,128)(2,1)S(1)} %multiply_convert_fusion.1, f32[1024,6,3,128]{0,3,2,1:T(8,128)} %copy-done.1, f32[6,128]{1,0:T(8,128)S(1)} %copy-done.5, f32[1024]{0:T(1024)S(1)} %get-tuple-element.29), kind=kOutput, calls=%fused_computation.56 | convolution fusion | flops 807665664 | bytes 16523264 | tf_op jit(solution)/shard_map/qhd,khd->hqk/dot_general | solution.py:93
  659.8 6.5 fusion.23
  666.2 17.4 %fusion.55 = (f32[6,512]{1,0:T(8,128)S(1)}, f32[6,512,1024]{2,1,0:T(8,128)}) fusion(f32[6,512,1024]{2,1,0:T(8,128)} %fusion.25, pred[512,1024]{1,0:T(8,128)(4,1)S(1)} %copy.93), kind=kOutput, calls=%fused_computation.124 | output fusion | flops 18875392 | bytes 25702400 | tf_op jit(solution)/shard_map/sub | solution.py:98
  683.6 7.0 fusion.21
  690.6 16.5 %fusion.54 = (f32[6,512]{1,0:T(8,128)S(1)}, f32[6,512,1024]{2,1,0:T(8,128)}) fusion(f32[6,512,1024]{2,1,0:T(8,128)} %fusion.23, pred[512,1024]{1,0:T(8,128)(4,1)S(1)} %copy-done.3), kind=kOutput, calls=%fused_computation.123 | output fusion | flops 18875392 | bytes 25702400 | tf_op jit(solution)/shard_map/sub | solution.py:98
  707.1 6.9 fusion.22
  715.4 3.3 copy.99
  718.7 2.8 convert_element_type.80
  721.5 2.0 convolution_convert_fusion.3
  725.5 45.3 %all_to_all.35 = bf16[8,2,64,768]{3,1,2,0:T(2,128)(2,1)S(1)} all-to-all(bf16[8,2,64,768]{3,1,2,0:T(2,128)(2,1)S(1)} %copy.100), channel_id=1, replica_groups=mesh['bal'=8,'seq'=4] {'bal'}, dimensions={0} | all-to-all | bytes 3145728 | tf_op jit(solution)/shard_map/all_to_all | solution.py:177
  771.9 22.5 %all_to_all.36 = bf16[8,2,64,768]{3,1,0,2:T(2,128)(2,1)S(1)} all-to-all(bf16[8,2,64,768]{3,1,0,2:T(2,128)(2,1)S(1)} %copy.101), channel_id=1, replica_groups=mesh['bal'=8,'seq'=4] {'seq'}, dimensions={2} | all-to-all | bytes 3145728 | tf_op jit(solution)/shard_map/all_to_all | solution.py:176
  (95 shorter events, 21.4 us)
Async XLA Ops:
  6.5 10.7 %copy-start.14 = (s32[16]{0:T(128)S(1)}, s32[16]{0:T(128)}, u32[]{:S(2)}) copy-start(s32[16]{0:T(128)} %param.12) | copy-start | bytes 196
  14.3 74.8 %collective-permute-start = (bf16[640,2304]{1,0:T(8,128)(2,1)}, bf16[640,2304]{1,0:T(8,128)(2,1)}, u32[]{:S(2)}, u32[]{:S(2)}) collective-permute-start(bf16[640,2304]{1,0:T(8,128)(2,1)} %copy.88), channel_id=1, source_target_pairs={{0,4},{4,8},{8,12},{12,16},{16,20},{20,24},{24,28},{28,0},{1,5},{5... | collective-permute-start | bytes 8847368 | tf_op jit(solution)/shard_map/ppermute | solution.py:29
  17.4 67.1 %copy-start.11 = (s32[16]{0:T(128)}, s32[16]{0:T(128)S(1)}, u32[]{:S(2)}) copy-start(s32[16]{0:T(128)S(1)} %multiply_add_fusion) | copy-start | bytes 196
  18.2 66.3 %all-to-all-start = ((bf16[8,1,2]{2,1,0:T(2,128)(2,1)}), bf16[8,1,2]{2,1,0:T(2,128)(2,1)S(1)}, u32[]{:S(2)}, u32[]{:S(2)}) async-start(bf16[8,1,2]{2,1,0:T(2,128)(2,1)} %all_to_all.30), calls=%async_computation | async-start | bytes 8192 | tf_op jit(solution)/shard_map/all_to_all | solution.py:122
  84.5 161.7 %all-to-all-start.1 = ((bf16[8,2,16,5120]{3,2,1,0:T(8,128)(2,1)}), bf16[8,2,16,5120]{3,2,1,0:T(8,128)(2,1)}, u32[]{:S(2)}, u32[]{:S(2)}) async-start(bf16[8,2,16,5120]{3,2,1,0:T(8,128)(2,1)} %bitcast.93), calls=%async_computation.1 | async-start | bytes 5242880 | tf_op jit(solution)/shard_map/all_to_all | solution.py:121
  89.0 164.3 %copy-start.13 = (s32[1,4,3]{1,0,2:T(1,128)S(1)}, s32[1,4,3]{1,0,2:T(1,128)}, u32[]{:S(2)}) copy-start(s32[1,4,3]{1,0,2:T(1,128)} %param.13) | copy-start | bytes 148
  89.0 502.1 %all-gather.2.cloned.1.call-start = ((), (), s32[]{:S(2)}) async-start(), calls=%async_computation.4 | async-start | bytes 13107200 | tf_op jit(solution)/shard_map/all_gather | solution.py:135
  89.0 154.4 %collective-permute-start.1 = (bf16[640,2304]{1,0:T(8,128)(2,1)}, bf16[640,2304]{1,0:T(8,128)(2,1)}, u32[]{:S(2)}, u32[]{:S(2)}) collective-permute-start(bf16[640,2304]{1,0:T(8,128)(2,1)} %collective-permute-done), channel_id=1, source_target_pairs={{0,4},{4,8},{8,12},{12,16},{16,20},{20,24},{24,28},{28,0},{1,5},{5... | collective-permute-start | bytes 8847368 | tf_op jit(solution)/shard_map/ppermute | solution.py:29
  90.9 162.5 %collective-permute-start.4 = (bf16[640,2304]{1,0:T(8,128)(2,1)}, bf16[640,2304]{1,0:T(8,128)(2,1)}, u32[]{:S(2)}, u32[]{:S(2)}) collective-permute-start(bf16[640,2304]{1,0:T(8,128)(2,1)} %copy.88), channel_id=1, source_target_pairs={{4,0},{8,4},{12,8},{16,12},{20,16},{24,20},{28,24},{0,28},{5,1},{9... | collective-permute-start | bytes 8847368 | tf_op jit(solution)/shard_map/ppermute | solution.py:32
  243.4 128.2 %collective-permute-start.2 = (bf16[640,2304]{1,0:T(8,128)(2,1)}, bf16[640,2304]{1,0:T(8,128)(2,1)}, u32[]{:S(2)}, u32[]{:S(2)}) collective-permute-start(bf16[640,2304]{1,0:T(8,128)(2,1)} %collective-permute-done.1), channel_id=1, source_target_pairs={{0,4},{4,8},{8,12},{12,16},{16,20},{20,24},{24,28},{28,0},{1,5},{5... | collective-permute-start | bytes 8847368 | tf_op jit(solution)/shard_map/ppermute | solution.py:29
  246.1 3.4 copy-start.9
  246.2 3.2 copy-start.6
  250.3 131.7 %copy-start.4 = (f32[1,4,2,5120]{3,2,1,0:T(2,128)S(1)}, f32[1,4,2,5120]{3,2,1,0:T(2,128)}, u32[]{:S(2)}) copy-start(f32[1,4,2,5120]{3,2,1,0:T(2,128)} %param.11) | copy-start | bytes 491524
  253.4 128.9 %collective-permute-start.5 = (bf16[640,2304]{1,0:T(8,128)(2,1)}, bf16[640,2304]{1,0:T(8,128)(2,1)}, u32[]{:S(2)}, u32[]{:S(2)}) collective-permute-start(bf16[640,2304]{1,0:T(8,128)(2,1)} %collective-permute-done.4), channel_id=1, source_target_pairs={{4,0},{8,4},{12,8},{16,12},{20,16},{24,20},{28,24},{0,28},{5,1},{9... | collective-permute-start | bytes 8847368 | tf_op jit(solution)/shard_map/ppermute | solution.py:32
  371.6 127.5 %collective-permute-start.3 = (bf16[640,2304]{1,0:T(8,128)(2,1)}, bf16[640,2304]{1,0:T(8,128)(2,1)}, u32[]{:S(2)}, u32[]{:S(2)}) collective-permute-start(bf16[640,2304]{1,0:T(8,128)(2,1)} %collective-permute-done.2), channel_id=1, source_target_pairs={{0,4},{4,8},{8,12},{12,16},{16,20},{20,24},{24,28},{28,0},{1,5},{5... | collective-permute-start | bytes 8847368 | tf_op jit(solution)/shard_map/ppermute | solution.py:29
  382.3 129.4 %collective-permute-start.6 = (bf16[640,2304]{1,0:T(8,128)(2,1)}, bf16[640,2304]{1,0:T(8,128)(2,1)S(1)}, u32[]{:S(2)}, u32[]{:S(2)}) collective-permute-start(bf16[640,2304]{1,0:T(8,128)(2,1)} %collective-permute-done.5), channel_id=1, source_target_pairs={{4,0},{8,4},{12,8},{16,12},{20,16},{24,20},{28,24},{0,28},{5,1},{9... | collective-permute-start | bytes 8847368 | tf_op jit(solution)/shard_map/ppermute | solution.py:32
  501.2 6.2 copy-start.2
  591.1 7.0 copy-start
  609.1 39.8 %copy-start.8 = (f32[6,128]{1,0:T(8,128)S(1)}, f32[6,128]{1,0:T(8,128)}, u32[]{:S(2)}) copy-start(f32[6,128]{1,0:T(8,128)} %param.9) | copy-start | bytes 9220
  638.8 3.6 copy-start.1
  642.5 8.8 %copy-start.5 = (f32[6,128]{1,0:T(8,128)S(1)}, f32[6,128]{1,0:T(8,128)}, u32[]{:S(2)}) copy-start(f32[6,128]{1,0:T(8,128)} %param.10) | copy-start | bytes 9220
  648.9 10.8 %slice-start = ((s8[9437184]{0:T(1024)(128)(4,1)}), s8[4194304]{0:T(1024)(128)(4,1)S(1)}, s32[]{:S(2)}) async-start(s8[9437184]{0:T(1024)(128)(4,1)} %bitcast.88), calls=%async_computation.5 | async-start | bytes 8388608
  651.3 8.4 %slice-start.1 = ((s8[9437184]{0:T(1024)(128)(4,1)}), s8[4194304]{0:T(1024)(128)(4,1)S(1)}, s32[]{:S(2)}) async-start(s8[9437184]{0:T(1024)(128)(4,1)} %bitcast.88), calls=%async_computation.6 | async-start | bytes 8388608
  651.3 8.4 %slice-start.2 = ((s8[9437184]{0:T(1024)(128)(4,1)}), s8[1048576]{0:T(1024)(128)(4,1)S(1)}, s32[]{:S(2)}) async-start(s8[9437184]{0:T(1024)(128)(4,1)} %bitcast.88), calls=%async_computation.7 | async-start | bytes 2097152
  683.6 7.0 copy-start.3
  714.0 7.5 copy-start.7
  714.1 7.5 copy-start.10
  725.5 71.4 %copy-start.12 = (s32[16]{0:T(128)S(1)}, s32[16]{0:T(128)}, u32[]{:S(2)}) copy-start(s32[16]{0:T(128)} %copy-done.11) | copy-start | bytes 196
Sparse Core Ops, SparseCore 0:
  253.4 69.8 all-gather.1
